TPU v7x, 128 devices: a whole 4x4x4 slice. The times are simulated.
128 devices in a mesh: seq: 16 (over z, y_lo, core), head: 8 (over x, y_hi).
Axes of the slice: x: 4, y: 4 (y_hi: 2, y_lo: 2; y = y_hi * 2 + y_lo), z: 4, core: 2. Of those that a mesh axis runs over, the one named last changes fastest.
Arguments:
- tokens: bfloat16 [128, 512, 1024], P('seq'), may hold values from -36 to 36
- lengths: int32 [128], P('seq'), may hold values from 1 to 512, 32768 in all
- attn_in: float32 [1024, 3, 1024], P(('seq', 'head')), may hold values from -0.4 to 0.4
- attn_out: float32 [1024, 1024], P(None, ('seq', 'head')), may hold values from -0.1875 to 0.1875
- mlp_in: float32 [1024, 4096], P(('seq', 'head')), may hold values from -0.1875 to 0.1875
- mlp_out: float32 [4096, 1024], P(None, ('seq', 'head')), may hold values from -0.09375 to 0.09375
- norm_gain: float32 [2, 1024], replicated, may hold values from 0.5 to 1.5
- norm_shift: float32 [2, 1024], replicated, may hold values from -3 to 3
Outputs:
- encoded: bfloat16 [128, 512, 1024], P('seq', 'head')
- key_cache: bfloat16 [128, 512, 1024], P('seq', None, 'head')
- value_cache: bfloat16 [128, 512, 1024], P('seq', None, 'head')
Inputs may be any that keep to these rules, and one draw needn't show every extreme that they name: `lengths`: some prompt has exactly 512 tokens.
All inputs are finite; a program needn't handle non-finite values. No bound on the sum of `lengths` on one device may be relied on, other than what follows from the above.
Results may differ from a plain program's by a relative error of at most 0.02.
Values may be sent and summed in bfloat16 or wider, within the bound.
A program may use at most 128 MiB of HBM per device.

v0:
```python
import math
import jax
import jax.numpy as jnp
from jax import lax
from jax.sharding import PartitionSpec as P

DH = 64
EPSILON = 1e-05


def layer_norm(values, gain, shift):
    center = values - jnp.mean(values, axis=-1, keepdims=True)
    spread = jnp.mean(center * center, axis=-1, keepdims=True)
    return center * lax.rsqrt(spread + EPSILON) * gain + shift


def shards(tokens, lengths, attn_in, attn_out, mlp_in, mlp_out, norm_gain, norm_shift):
    heads_axis = lax.axis_size("head")
    head_index = lax.axis_index("head")
    prompts = tokens.shape[0]
    seq_len = tokens.shape[1]
    model_width = tokens.shape[2]
    hidden_width = mlp_in.shape[1]
    block_width = model_width // heads_axis
    hidden_block = hidden_width // heads_axis
    local_heads = block_width // DH
    in_cast = attn_in.astype(jnp.bfloat16)
    up_cast = mlp_in.astype(jnp.bfloat16)
    out_cast = attn_out.astype(jnp.bfloat16)
    down_cast = mlp_out.astype(jnp.bfloat16)
    whole_in, whole_up = (
        lax.all_gather(in_cast, ("seq", "head"), axis=0, tiled=True),
        lax.all_gather(up_cast, ("seq", "head"), axis=0, tiled=True),
    )
    whole_out, whole_down = (
        lax.all_gather(out_cast, ("seq", "head"), axis=1, tiled=True),
        lax.all_gather(down_cast, ("seq", "head"), axis=1, tiled=True),
    )
    qkv_weight = lax.dynamic_slice_in_dim(whole_in, head_index * block_width, block_width, 2)
    up_weight = lax.dynamic_slice_in_dim(whole_up, head_index * hidden_block, hidden_block, 1)
    proj_weight = lax.dynamic_slice_in_dim(whole_out, head_index * block_width, block_width, 0)
    down_weight = lax.dynamic_slice_in_dim(whole_down, head_index * hidden_block, hidden_block, 0)
    projected = jnp.einsum(
        "pld,dte->plte", tokens, qkv_weight, preferred_element_type=jnp.float32
    ).astype(jnp.bfloat16)
    positions = jnp.arange(seq_len, dtype=jnp.int32)
    inside = positions[None, :] < lengths[:, None]
    key_part = projected[:, :, 1]
    value_part = projected[:, :, 2]
    queries = projected[:, :, 0].reshape(prompts, seq_len, local_heads, DH)
    key_heads = key_part.reshape(prompts, seq_len, local_heads, DH)
    value_heads = value_part.reshape(prompts, seq_len, local_heads, DH)
    scores = jnp.einsum(
        "pqhd,pkhd->phqk", queries, key_heads, preferred_element_type=jnp.float32
    ) * (1.0 / math.sqrt(DH))
    scores = jnp.where(inside[:, None, None, :], scores, -1e30)
    row_peak = jnp.max(scores, axis=-1, keepdims=True)
    raised = jnp.exp(scores - row_peak)
    weights = (raised / jnp.sum(raised, axis=-1, keepdims=True)).astype(jnp.bfloat16)
    context = jnp.einsum(
        "phqk,pkhd->pqhd", weights, value_heads, preferred_element_type=jnp.float32
    )
    context = context.astype(jnp.bfloat16).reshape(prompts, seq_len, block_width)
    key_cache = jnp.where(inside[:, :, None], key_part, jnp.zeros_like(key_part))
    value_cache = jnp.where(inside[:, :, None], value_part, jnp.zeros_like(value_part))
    row_count = seq_len // heads_axis
    row_start = head_index * row_count
    attn_partial = jnp.einsum(
        "pld,de->ple", context, proj_weight, preferred_element_type=jnp.float32
    )
    attn_total = lax.psum(attn_partial.astype(jnp.bfloat16), "head").astype(jnp.float32)
    normed = layer_norm(
        tokens.astype(jnp.float32) + attn_total, norm_gain[0], norm_shift[0]
    ).astype(jnp.bfloat16)
    hidden = jax.nn.gelu(
        jnp.einsum("pld,df->plf", normed, up_weight, preferred_element_type=jnp.float32),
        approximate=False,
    ).astype(jnp.bfloat16)
    mlp_partial = jnp.einsum("plf,fe->ple", hidden, down_weight, preferred_element_type=jnp.float32)
    mlp_total = lax.psum(mlp_partial.astype(jnp.bfloat16), "head").astype(jnp.float32)
    mlp_rows = lax.dynamic_slice_in_dim(mlp_total, row_start, row_count, 1)
    normed_rows = lax.dynamic_slice_in_dim(normed, row_start, row_count, 1)
    finished = layer_norm(normed_rows.astype(jnp.float32) + mlp_rows, norm_gain[1], norm_shift[1])
    inside_rows = lax.dynamic_slice_in_dim(inside, row_start, row_count, 1)
    encoded = jnp.where(inside_rows[:, :, None], finished, 0.0).astype(jnp.bfloat16)
    return (encoded, key_cache, value_cache)


def solution(mesh):
    in_specs = (
        P("seq", None, None),
        P("seq"),
        P(("seq", "head"), None, None),
        P(None, ("seq", "head")),
        P(("seq", "head"), None),
        P(None, ("seq", "head")),
        P(),
        P(),
    )
    out_specs = (P("seq", "head", None), P("seq", None, "head"), P("seq", None, "head"))
    return jax.shard_map(shards, mesh=mesh, in_specs=in_specs, out_specs=out_specs, check_vma=False)
```

profile of v0, /device:TPU:5, one launch (start us, length us, event | category | flops | bytes accessed | tf_op | source)
XLA Modules:
  0.0 1998.5 jit_solution(4811427423601753310)
XLA Ops:
  7.2 1.5 convert_element_type.55
  8.8 0.0 all-gather.7.cloned.1.call-start
  8.8 1.4 convert_element_type.61
  10.2 0.7 iota_compare_fusion
  11.0 312.5 %all-gather.5.cloned.1.call-done = bf16[1024,3,1024]{2,0,1:T(8,128)(2,1)} async-done(((bf16[8,3,1024]{2,0,1:T(8,128)(2,1)}), bf16[1024,3,1024]{2,0,1:T(8,128)(2,1)}) %all-gather.5.cloned.1.call-update) | async-done | bytes 6291472 | tf_op jit(solution)/shard_map/all_gather | solution.py:32
  323.5 7.1 convert_bitcast_fusion
  330.6 1.7 fusion.108
  332.4 10.7 fusion.111
  343.1 8.7 fusion.59
  351.8 275.5 %all-gather.7.cloned.1.call-done = bf16[1024,1024]{0,1:T(8,128)(2,1)} async-done(((bf16[1024,8]{0,1:T(8,128)(2,1)}), bf16[1024,1024]{0,1:T(8,128)(2,1)}) %all-gather.7.cloned.1.call-update) | async-done | bytes 2097168 | tf_op jit(solution)/shard_map/all_gather | solution.py:36
  627.3 6.9 convolution_convert_fusion
  634.3 0.0 all-gather.9.cloned.1.call-start
  634.3 0.6 convert_element_type.66
  635.1 0.6 convert_element_type.68
  635.7 0.2 all-reduce.5.cloned.1.call-start
  636.0 347.3 %all-reduce.3.cloned.1.call-done = bf16[8,512,1024]{2,1,0:T(8,128)(2,1)} async-done(((bf16[8,512,1024]{2,1,0:T(8,128)(2,1)}), bf16[8,512,1024]{2,1,0:T(8,128)(2,1)}) %all-reduce.3.cloned.1.call-update) | async-done | bytes 8388624 | tf_op jit(solution)/shard_map/psum | solution.py:71
  983.3 8.0 fusion.2
  991.3 8.0 multiply_reduce_fusion
  999.4 0.3 copy-done
  999.7 9.3 add_convert_fusion
  1009.0 286.9 %all-gather.9.cloned.1.call-done = bf16[1024,4096]{1,0:T(8,128)(2,1)} async-done(((bf16[8,4096]{1,0:T(8,128)(2,1)}), bf16[1024,4096]{1,0:T(8,128)(2,1)}) %all-gather.9.cloned.1.call-update) | async-done | bytes 8388624 | tf_op jit(solution)/shard_map/all_gather | solution.py:33
  1295.8 14.5 fusion.54
  1310.3 300.0 %all-gather.11.cloned.1.call-done = bf16[4096,1024]{0,1:T(8,128)(2,1)} async-done(((bf16[4096,8]{0,1:T(8,128)(2,1)}), bf16[4096,1024]{0,1:T(8,128)(2,1)}) %all-gather.11.cloned.1.call-update) | async-done | bytes 8388624 | tf_op jit(solution)/shard_map/all_gather | solution.py:37
  1610.4 25.3 %convolution_convert_fusion.1 = bf16[8,512,1024]{2,1,0:T(8,128)(2,1)} fusion(f32[8,512,512]{2,1,0:T(8,128)} %get-tuple-element.22, u8[512,512]{1,0:T(8,128)(4,1)} %get-tuple-element.10, u8[512,512]{1,0:T(8,128)(4,1)} %get-tuple-element.9, bf16[4096,1024]{0,1:T(8,128)(2,1)} %all-gather.11.cloned.1.call-done, s32[]{:T(128)S(6)} %select_n.31), kind=kOutput, calls=%fused_computation.39 | convolution fusion | flops 4445962240 | bytes 18350084 | tf_op jit(solution)/shard_map/plf,fe->ple/dot_general | solution.py:79
  1635.7 0.1 constant_dynamic-slice_fusion
  1635.8 1.5 bitcast_select_fusion
  1637.2 2.3 copy.23
  1639.5 2.3 copy.24
  1641.8 342.7 %all-reduce.5.cloned.1.call-done = bf16[8,512,1024]{2,1,0:T(8,128)(2,1)} async-done(((bf16[8,512,1024]{2,1,0:T(8,128)(2,1)}), bf16[8,512,1024]{2,1,0:T(8,128)(2,1)}) %all-reduce.5.cloned.1.call-update) | async-done | bytes 8388624 | tf_op jit(solution)/shard_map/psum | solution.py:80
  1984.4 1.9 fusion.56
  1986.3 2.0 multiply_reduce_fusion.1
  1988.4 3.2 select_convert_fusion
  (24 shorter events, 0.3 us)
Async XLA Ops:
  7.2 316.3 %all-gather.5.cloned.1.call-start = ((), (), s32[]{:S(2)}) async-start(), calls=%async_computation | async-start | bytes 6340608 | tf_op jit(solution)/shard_map/all_gather | solution.py:32
  8.8 618.6 %all-gather.7.cloned.1.call-start = ((), (), s32[]{:S(2)}) async-start(), calls=%async_computation.1 | async-start | bytes 2113536 | tf_op jit(solution)/shard_map/all_gather | solution.py:36
  10.2 973.1 %all-reduce.3.cloned.1.call-start = ((), (), s32[]{:S(2)}) async-start(), calls=%async_computation.2 | async-start | bytes 16777216 | tf_op jit(solution)/shard_map/psum | solution.py:71
  627.3 7.0 copy-start.1
  627.3 7.7 copy-start.2
  627.3 8.6 copy-start.3
  627.3 8.6 copy-start.4
  634.3 661.5 %all-gather.9.cloned.1.call-start = ((), (), s32[]{:S(2)}) async-start(), calls=%async_computation.3 | async-start | bytes 8454144 | tf_op jit(solution)/shard_map/all_gather | solution.py:33
  635.0 975.4 %all-gather.11.cloned.1.call-start = ((), (), s32[]{:S(2)}) async-start(), calls=%async_computation.4 | async-start | bytes 8454144 | tf_op jit(solution)/shard_map/all_gather | solution.py:37
  635.7 1348.7 %all-reduce.5.cloned.1.call-start = ((), (), s32[]{:S(2)}) async-start(), calls=%async_computation.5 | async-start | bytes 16777216 | tf_op jit(solution)/shard_map/psum | solution.py:80
  991.3 8.4 copy-start
Sparse Core Ops, SparseCore 0:
  10.3 313.1 all-gather.4
  325.2 302.0 all-gather.6
  634.4 348.8 all-reduce.2
  985.4 310.3 all-gather.8
  1297.9 312.4 all-gather.10
  1635.8 348.5 all-reduce.4
where the time goes:
time: 2000 us
  waiting for transfers between devices  1870 us (94%)
  matrix products  73.3 us (4%)
  other arithmetic  38.8 us (2%)
    psum x1, waiting for transfers between devices, shards(): lax.psum(attn_partial.astype(jnp.bfloat16), 'head').astype(jnp.float32)  347 us
    psum x1, waiting for transfers between devices, shards(): lax.psum(mlp_partial.astype(jnp.bfloat16), 'head').astype(jnp.float32)  343 us
    all_gather x1, waiting for transfers between devices, shards(): lax.all_gather(in_cast, ('seq', 'head'), axis=0, tiled=True)  313 us
    all_gather x1, waiting for transfers between devices, shards(): lax.all_gather(down_cast, ('seq', 'head'), axis=1, tiled=True)  300 us
    all_gather x1, waiting for transfers between devices, shards(): lax.all_gather(up_cast, ('seq', 'head'), axis=0, tiled=True)  287 us
    all_gather x1, waiting for transfers between devices, shards(): lax.all_gather(out_cast, ('seq', 'head'), axis=1, tiled=True)  276 us
  transfers between devices with their start and end apart: 6, of which 6 were waited for; matrix products, arithmetic and copies ran while one was open for 4% of the time, Pallas kernels for 0%

commit v1 on v0

--- a/solution.py
+++ b/solution.py
@@ -68,7 +68,9 @@
     attn_partial = jnp.einsum(
         "pld,de->ple", context, proj_weight, preferred_element_type=jnp.float32
     )
-    attn_total = lax.psum(attn_partial.astype(jnp.bfloat16), "head").astype(jnp.float32)
+    attn_total = jnp.sum(lax.all_gather(attn_partial.astype(jnp.bfloat16), "head"), axis=0).astype(
+        jnp.float32
+    )
     normed = layer_norm(
         tokens.astype(jnp.float32) + attn_total, norm_gain[0], norm_shift[0]
     ).astype(jnp.bfloat16)

time: 2000 us -> 2300 us (1.15)
  waiting for transfers between devices: 1870 us -> 2140 us
  other arithmetic: 38.8 us -> 64.9 us
    all_gather x0 -> x1, waiting for transfers between devices: none -> 646 us  [shards(): lax.all_gather(attn_partial.astype(jnp.bfloat16), 'head')]
    psum x1 -> x0, waiting for transfers between devices: 347 us -> none  [shards(): lax.psum(attn_partial.astype(jnp.bfloat16), 'head').astype(jnp.float32)]
    reduce_sum x0 -> x1, other arithmetic: none -> 26 us  [shards(): jnp.sum(lax.all_gather(attn_partial.astype(jnp.bfloat16), 'head'), axis=0)]
    all_gather x1, waiting for transfers between devices: 287 us -> 262 us  [shards(): lax.all_gather(up_cast, ('seq', 'head'), axis=0, tiled=True)]
  transfers between devices with their start and end apart: 6 -> 6, of which waited for: 6 -> 6; matrix products, arithmetic and copies ran while one was open for 4% -> 5% of each run, Pallas kernels for 0% -> 0%
where the time goes in v1:
time: 2300 us
  waiting for transfers between devices  2140 us (93%)
  matrix products  73.3 us (3%)
  other arithmetic  64.9 us (3%)
    all_gather x1, waiting for transfers between devices, shards(): lax.all_gather(attn_partial.astype(jnp.bfloat16), 'head')  646 us
    psum x1, waiting for transfers between devices, shards(): lax.psum(mlp_partial.astype(jnp.bfloat16), 'head').astype(jnp.float32)  343 us
    all_gather x1, waiting for transfers between devices, shards(): lax.all_gather(in_cast, ('seq', 'head'), axis=0, tiled=True)  313 us
    all_gather x1, waiting for transfers between devices, shards(): lax.all_gather(down_cast, ('seq', 'head'), axis=1, tiled=True)  300 us
    all_gather x1, waiting for transfers between devices, shards(): lax.all_gather(out_cast, ('seq', 'head'), axis=1, tiled=True)  276 us
    all_gather x1, waiting for transfers between devices, shards(): lax.all_gather(up_cast, ('seq', 'head'), axis=0, tiled=True)  262 us
  transfers between devices with their start and end apart: 6, of which 6 were waited for; matrix products, arithmetic and copies ran while one was open for 5% of the time, Pallas kernels for 0%

profile of v1, /device:TPU:5, one launch (start us, length us, event | category | flops | bytes accessed | tf_op | source)
XLA Modules:
  0.0 2298.1 jit_solution(7242184168369301390)
XLA Ops:
  7.2 1.5 convert_element_type.57
  8.8 0.0 all-gather.9.cloned.1.call-start
  8.8 1.4 convert_element_type.63
  10.2 0.7 iota_compare_fusion
  11.0 312.5 %all-gather.7.cloned.1.call-done = bf16[1024,3,1024]{2,0,1:T(8,128)(2,1)} async-done(((bf16[8,3,1024]{2,0,1:T(8,128)(2,1)}), bf16[1024,3,1024]{2,0,1:T(8,128)(2,1)}) %all-gather.7.cloned.1.call-update) | async-done | bytes 6291472 | tf_op jit(solution)/shard_map/all_gather | solution.py:32
  323.5 7.1 convert_bitcast_fusion
  330.6 1.7 fusion.108
  332.4 10.7 fusion.111
  343.1 8.7 fusion.59
  351.8 275.5 %all-gather.9.cloned.1.call-done = bf16[1024,1024]{0,1:T(8,128)(2,1)} async-done(((bf16[1024,8]{0,1:T(8,128)(2,1)}), bf16[1024,1024]{0,1:T(8,128)(2,1)}) %all-gather.9.cloned.1.call-update) | async-done | bytes 2097168 | tf_op jit(solution)/shard_map/all_gather | solution.py:36
  627.3 6.9 convolution_convert_fusion
  634.3 0.6 convert_element_type.68
  635.0 0.6 convert_element_type.70
  635.7 0.2 all-reduce.2.cloned.1.call-start
  636.0 645.8 %all-gather.15.cloned.1.call-done = bf16[64,512,1024]{2,1,0:T(8,128)(2,1)} async-done(((bf16[8,512,1024]{2,1,0:T(8,128)(2,1)}), bf16[64,512,1024]{2,1,0:T(8,128)(2,1)}) %all-gather.15.cloned.1.call-update) | async-done | bytes 67108880 | tf_op jit(solution)/shard_map/all_gather | solution.py:71
  1281.8 26.0 %reduce_sum.58 = bf16[8,512,1024]{2,1,0:T(8,128)(2,1)} reduce(bf16[8,8,512,1024]{3,2,1,0:T(8,128)(2,1)} %bitcast.10, bf16[]{:T(256)} %constant.12.clone.1), dimensions={0}, to_apply=%region_2.3 | reduce | flops 29360128 | bytes 75497472 | tf_op jit(solution)/shard_map/reduce_sum | solution.py:71
  1307.8 8.1 fusion.2
  1315.9 8.1 multiply_reduce_fusion
  1324.0 0.3 copy-done
  1324.2 9.2 add_convert_fusion
  1333.5 262.0 %all-gather.11.cloned.1.call-done = bf16[1024,4096]{1,0:T(8,128)(2,1)} async-done(((bf16[8,4096]{1,0:T(8,128)(2,1)}), bf16[1024,4096]{1,0:T(8,128)(2,1)}) %all-gather.11.cloned.1.call-update) | async-done | bytes 8388624 | tf_op jit(solution)/shard_map/all_gather | solution.py:33
  1595.5 14.5 fusion.54
  1610.0 300.0 %all-gather.13.cloned.1.call-done = bf16[4096,1024]{0,1:T(8,128)(2,1)} async-done(((bf16[4096,8]{0,1:T(8,128)(2,1)}), bf16[4096,1024]{0,1:T(8,128)(2,1)}) %all-gather.13.cloned.1.call-update) | async-done | bytes 8388624 | tf_op jit(solution)/shard_map/all_gather | solution.py:37
  1910.0 25.3 %convolution_convert_fusion.1 = bf16[8,512,1024]{2,1,0:T(8,128)(2,1)} fusion(f32[8,512,512]{2,1,0:T(8,128)} %get-tuple-element.22, u8[512,512]{1,0:T(8,128)(4,1)} %get-tuple-element.10, u8[512,512]{1,0:T(8,128)(4,1)} %get-tuple-element.9, bf16[4096,1024]{0,1:T(8,128)(2,1)} %all-gather.13.cloned.1.call-done, s32[]{:T(128)S(6)} %select_n.31), kind=kOutput, calls=%fused_computation.39 | convolution fusion | flops 4445962240 | bytes 18350084 | tf_op jit(solution)/shard_map/plf,fe->ple/dot_general | solution.py:81
  1935.4 0.1 constant_dynamic-slice_fusion
  1935.4 1.5 bitcast_select_fusion
  1936.9 2.3 copy.23
  1939.2 2.3 copy.24
  1941.4 342.7 %all-reduce.2.cloned.1.call-done = bf16[8,512,1024]{2,1,0:T(8,128)(2,1)} async-done(((bf16[8,512,1024]{2,1,0:T(8,128)(2,1)}), bf16[8,512,1024]{2,1,0:T(8,128)(2,1)}) %all-reduce.2.cloned.1.call-update) | async-done | bytes 8388624 | tf_op jit(solution)/shard_map/psum | solution.py:82
  2284.1 1.9 fusion.56
  2286.0 2.0 multiply_reduce_fusion.1
  2288.0 3.2 select_convert_fusion
  (25 shorter events, 0.3 us)
Async XLA Ops:
  7.2 316.3 %all-gather.7.cloned.1.call-start = ((), (), s32[]{:S(2)}) async-start(), calls=%async_computation | async-start | bytes 6340608 | tf_op jit(solution)/shard_map/all_gather | solution.py:32
  8.8 618.6 %all-gather.9.cloned.1.call-start = ((), (), s32[]{:S(2)}) async-start(), calls=%async_computation.1 | async-start | bytes 2113536 | tf_op jit(solution)/shard_map/all_gather | solution.py:36
  10.2 1271.6 %all-gather.15.cloned.1.call-start = ((), (), s32[]{:S(2)}) async-start(), calls=%async_computation.5 | async-start | bytes 75497472 | tf_op jit(solution)/shard_map/all_gather | solution.py:71
  627.3 7.0 copy-start.1
  627.3 7.7 copy-start.2
  627.3 8.6 copy-start.3
  627.3 8.6 copy-start.4
  634.2 961.2 %all-gather.11.cloned.1.call-start = ((), (), s32[]{:S(2)}) async-start(), calls=%async_computation.2 | async-start | bytes 8454144 | tf_op jit(solution)/shard_map/all_gather | solution.py:33
  635.0 1275.1 %all-gather.13.cloned.1.call-start = ((), (), s32[]{:S(2)}) async-start(), calls=%async_computation.3 | async-start | bytes 8454144 | tf_op jit(solution)/shard_map/all_gather | solution.py:37
  635.7 1648.4 %all-reduce.2.cloned.1.call-start = ((), (), s32[]{:S(2)}) async-start(), calls=%async_computation.4 | async-start | bytes 16777216 | tf_op jit(solution)/shard_map/psum | solution.py:82
  1315.9 8.4 copy-start
Sparse Core Ops, SparseCore 0:
  10.3 313.1 all-gather.6
  325.2 302.0 all-gather.8
  634.4 647.3 all-gather.14
  1283.9 311.5 all-gather.10
  1597.6 312.3 all-gather.12
  1935.5 348.5 all-reduce.1
